TPU v7x, 512 devices: a whole 4x8x8 slice. The times are simulated.
512 devices in a mesh: dp: 16 (over y, core), seq: 32 (over x, z).
Axes of the slice: x: 4, y: 8, z: 8, core: 2. Of those that a mesh axis runs over, the one named last changes fastest.
Arguments:
- queries: bfloat16 [16, 4096, 2048], P('dp', 'seq'), may hold values from -40 to 40, as said below
- keys: bfloat16 [16, 4096, 2048], P('dp', 'seq'), may hold values from -40 to 40, as said below
- values: bfloat16 [16, 4096, 2048], P('dp', 'seq'), may hold values from -40 to 40, as said below
- gain: float32 [2048], replicated, may hold values from 0.1 to 1.9
- cotangent: bfloat16 [16, 4096, 2048], P('dp', 'seq'), may hold values from -240 to 240, as said below
Outputs:
- output: bfloat16 [16, 4096, 2048], P('dp', 'seq')
- grad_query: bfloat16 [16, 4096, 2048], P('dp', 'seq')
- grad_key: bfloat16 [16, 4096, 2048], P('dp', 'seq')
- grad_value: bfloat16 [16, 4096, 2048], P('dp', 'seq')
- gain_grad: float32 [2048], replicated
Inputs may be any that keep to these rules, and one draw needn't show every extreme that they name: queries: independent entries with row and feature scales. keys: independent entries with row and feature scales. values: independent entries with row and feature scales. cotangent: independent entries with row and feature scales.
All inputs are finite; a program needn't handle non-finite values.
Results may differ from a plain program's by a relative error of at most 0.0058.
Values may be sent and summed in bfloat16 or wider, within the bound.
A program may use at most 64 MiB of HBM per device.

v0:
```python
import jax
import jax.numpy as jnp
from jax import lax
from jax.sharding import PartitionSpec as P

HEADS = 16
EPSILON = 1e-06


def prefix_swapped(state_block, reverse_order):
    device_count = lax.axis_size("seq")
    flat_state = state_block.reshape(1, -1)
    columns = lax.all_to_all(flat_state, "seq", split_axis=1, concat_axis=0, tiled=True)
    device_rank = jnp.arange(device_count)
    if reverse_order:
        triangle = device_rank[None, :] > device_rank[:, None]
    else:
        triangle = device_rank[None, :] < device_rank[:, None]
    summed = jnp.dot(triangle.astype(jnp.float32), columns, precision=lax.Precision.HIGHEST)
    summed_half = summed.astype(jnp.bfloat16)
    returned = lax.all_to_all(summed_half, "seq", split_axis=0, concat_axis=1, tiled=True)
    return returned.reshape(state_block.shape)


def per_device(queries, keys, values, gain, cotangent):
    row_count = queries.shape[1]
    feature_count = queries.shape[2]
    head_size = feature_count // HEADS
    scaling = head_size ** (-0.5)
    query_rows = queries[0].reshape(row_count, HEADS, head_size)
    key_rows = keys[0].reshape(row_count, HEADS, head_size)
    value_rows = values[0].reshape(row_count, HEADS, head_size)
    kv_local = jnp.einsum("thd,the->hde", key_rows, value_rows, preferred_element_type=jnp.float32)
    prefix_half = prefix_swapped(kv_local, False)
    position = jnp.arange(row_count)
    causal_mask = (position[:, None] >= position[None, :]).astype(jnp.float32)
    scores = (
        jnp.einsum("thd,uhd->htu", query_rows, key_rows, preferred_element_type=jnp.float32)
        * scaling
        * causal_mask
    ).astype(jnp.bfloat16)
    attended = jnp.einsum("htu,uhe->the", scores, value_rows, preferred_element_type=jnp.float32)
    attended = attended + scaling * jnp.einsum(
        "thd,hde->the", query_rows, prefix_half, preferred_element_type=jnp.float32
    )
    attended = attended.reshape(row_count, feature_count)
    root_mean = jnp.sqrt(jnp.mean(attended * attended, axis=-1, keepdims=True) + EPSILON)
    normalized = attended / root_mean
    output = (gain * normalized).astype(jnp.bfloat16)[None]
    upstream = cotangent[0].astype(jnp.float32)
    partial_gain = jnp.sum(upstream * normalized, axis=0)
    total_gain = lax.psum(partial_gain, ("dp", "seq"))
    gain_grad = total_gain / lax.axis_size("dp")
    scaled = upstream * gain
    inner_mean = jnp.mean(scaled * normalized, axis=-1, keepdims=True)
    grad_attn = (
        ((scaled - normalized * inner_mean) / root_mean)
        .astype(jnp.bfloat16)
        .reshape(row_count, HEADS, head_size)
    )
    local_grads = scaling * jnp.einsum(
        "thd,the->hde", query_rows, grad_attn, preferred_element_type=jnp.float32
    )
    suffix_half = prefix_swapped(local_grads, True)
    grad_scores = (
        jnp.einsum("the,uhe->htu", grad_attn, value_rows, preferred_element_type=jnp.float32)
        * causal_mask
    ).astype(jnp.bfloat16)
    grad_query = scaling * (
        jnp.einsum("htu,uhd->thd", grad_scores, key_rows, preferred_element_type=jnp.float32)
        + jnp.einsum("the,hde->thd", grad_attn, prefix_half, preferred_element_type=jnp.float32)
    )
    grad_key = scaling * jnp.einsum(
        "htu,thd->uhd", grad_scores, query_rows, preferred_element_type=jnp.float32
    ) + jnp.einsum("uhe,hde->uhd", value_rows, suffix_half, preferred_element_type=jnp.float32)
    grad_value = jnp.einsum(
        "htu,the->uhe", scores, grad_attn, preferred_element_type=jnp.float32
    ) + jnp.einsum("uhd,hde->uhe", key_rows, suffix_half, preferred_element_type=jnp.float32)
    out_shape = (1, row_count, feature_count)
    return (
        output,
        grad_query.reshape(out_shape).astype(jnp.bfloat16),
        grad_key.reshape(out_shape).astype(jnp.bfloat16),
        grad_value.reshape(out_shape).astype(jnp.bfloat16),
        gain_grad,
    )


def solution(mesh):
    return jax.shard_map(
        per_device,
        mesh=mesh,
        in_specs=(
            P("dp", "seq", None),
            P("dp", "seq", None),
            P("dp", "seq", None),
            P(),
            P("dp", "seq", None),
        ),
        out_specs=(
            P("dp", "seq", None),
            P("dp", "seq", None),
            P("dp", "seq", None),
            P("dp", "seq", None),
            P(),
        ),
        check_vma=False,
    )
```

profile of v0, /device:TPU:1, one launch (start us, length us, event | category | flops | bytes accessed | tf_op | source)
XLA Modules:
  0.0 252.3 jit_solution(6267400844076144092)
XLA Ops:
  0.6 1.1 copy.128
  3.4 38.4 %all_to_all.58 = f32[1,32,8192]{2,0,1:T(1,128)S(1)} all-to-all(f32[1,32,8192]{2,0,1:T(1,128)S(1)} %bitcast.94), channel_id=1, replica_groups=mesh['dp'=16,'seq'=32] {'seq'}, dimensions={1} | all-to-all | bytes 2097152 | tf_op jit(solution)/shard_map/all_to_all | solution.py:13
  41.7 1.3 fusion
  43.5 1.0 reduce.3
  44.6 1.2 reshape.208
  45.7 8.5 %all-to-all-start.1 = ((bf16[32,2,4096]{2,1,0:T(2,128)(2,1)}), bf16[32,2,4096]{2,1,0:T(2,128)(2,1)S(1)}, u32[]{:S(2)}, u32[]{:S(2)}) async-start(bf16[32,2,4096]{2,1,0:T(2,128)(2,1)} %reshape.208), calls=%async_computation.1 | async-start | bytes 1048576 | tf_op jit(solution)/shard_map/all_to_all | solution.py:21
  55.3 1.2 copy.99
  57.0 1.5 convolution_bitcast_fusion.3
  58.5 9.7 %all-to-all-done.1 = bf16[32,2,4096]{2,1,0:T(2,128)(2,1)S(1)} async-done(((bf16[32,2,4096]{2,1,0:T(2,128)(2,1)}), bf16[32,2,4096]{2,1,0:T(2,128)(2,1)S(1)}, u32[]{:S(2)}, u32[]{:S(2)}) %all-to-all-start.1) | async-done | bytes 524320 | tf_op jit(solution)/shard_map/all_to_all | solution.py:21
  68.7 4.0 %reduce.1 = bf16[32,8192]{1,0:T(8,128)(2,1)} reduce(bf16[32,1,8192]{2,1,0:T(2,128)(2,1)S(1)} %reshape.209, bf16[]{:T(256)} %constant.19), dimensions={1}, to_apply=%all_to_all.48.reduce_sub_computation | reduce | bytes 1048578 | tf_op jit(solution)/shard_map/all_to_all | solution.py:21
  72.7 1.3 reshape.200
  74.0 1.9 multiply_reduce_fusion
  75.9 1.4 copy.100
  77.3 1.7 fusion.20
  79.4 1.3 fusion.3
  80.7 2.5 %copy.108 = f32[16,128,128]{2,1,0:T(8,128)} copy(f32[16,128,128]{1,2,0:T(8,128)} %fusion.3) | data formatting | bytes 2097152 | tf_op jit(solution)/shard_map/mul | solution.py:61
  83.2 8.1 %all-to-all-start.2 = ((f32[1,32,8192]{2,0,1:T(1,128)}), f32[1,32,8192]{2,0,1:T(1,128)}, u32[]{:S(2)}, u32[]{:S(2)}) async-start(f32[1,32,8192]{2,0,1:T(1,128)} %bitcast.93), calls=%async_computation.2 | async-start | bytes 2097152 | tf_op jit(solution)/shard_map/all_to_all | solution.py:13
  93.6 1.1 fusion.9
  94.7 21.5 %all-to-all-done.2 = f32[1,32,8192]{2,0,1:T(1,128)} async-done(((f32[1,32,8192]{2,0,1:T(1,128)}), f32[1,32,8192]{2,0,1:T(1,128)}, u32[]{:S(2)}, u32[]{:S(2)}) %all-to-all-start.2) | async-done | bytes 1048608 | tf_op jit(solution)/shard_map/all_to_all | solution.py:13
  116.2 3.2 %fusion.1 = bf16[32,1,8192]{2,0,1:T(8,128)(2,1)} fusion(f32[1,32,8192]{2,0,1:T(1,128)} %all-to-all-done.2), kind=kOutput, calls=%fused_computation.3 | convolution fusion | flops 100926464 | bytes 1572864 | tf_op jit(solution)/shard_map/dot_general | solution.py:19
  119.4 2.7 %reduce.4 = bf16[32,8192]{1,0:T(8,128)(2,1)} reduce(bf16[32,1,8192]{2,0,1:T(8,128)(2,1)} %fusion.1, bf16[]{:T(256)} %broadcast.107), dimensions={1}, to_apply=%copy.110.reduce_sub_computation | reduce | bytes 1048578 | tf_op jit(solution)/shard_map/all_to_all | solution.py:21
  122.1 2.2 reshape.210
  124.3 8.3 %all-to-all-start.3 = ((bf16[32,2,4096]{2,1,0:T(2,128)(2,1)}), bf16[32,2,4096]{2,1,0:T(2,128)(2,1)}, u32[]{:S(2)}, u32[]{:S(2)}) async-start(bf16[32,2,4096]{2,1,0:T(2,128)(2,1)} %reshape.210), calls=%async_computation.3 | async-start | bytes 1048576 | tf_op jit(solution)/shard_map/all_to_all | solution.py:21
  132.6 2.4 fusion.4
  135.0 1.4 copy.98
  136.3 1.0 copy.116
  137.4 99.2 %psum.7 = f32[2048]{0:T(1024)S(1)} all-reduce(f32[2048]{0:T(1024)S(1)} %get-tuple-element.25), channel_id=1, replica_groups=mesh['dp'=16,'seq'=32] {'dp','seq'}, use_global_device_ids=true, to_apply=%region_3.0 | all-reduce | flops 2048 | bytes 16384 | tf_op jit(solution)/shard_map/psum | solution.py:52
  239.4 3.6 %reshape.211 = bf16[32,1,8192]{2,1,0:T(2,128)(2,1)S(1)} reshape(bf16[32,2,4096]{2,1,0:T(2,128)(2,1)} %all-to-all-done.3) | data formatting | bytes 1048576
  243.0 4.0 %reduce.2 = bf16[32,8192]{1,0:T(8,128)(2,1)} reduce(bf16[32,1,8192]{2,1,0:T(2,128)(2,1)S(1)} %reshape.211, bf16[]{:T(256)} %constant.19), dimensions={1}, to_apply=%all_to_all.53.reduce_sub_computation | reduce | bytes 1048578 | tf_op jit(solution)/shard_map/all_to_all | solution.py:21
  246.9 1.3 reshape.203
  250.2 1.0 copy.117
  251.2 1.0 copy.118
  (53 shorter events, 11.6 us)
Async XLA Ops:
  1.8 1.0 copy-start.13
  2.3 0.8 copy-start.3
  45.7 8.5 %copy-start.14 = (bf16[1,128,2048]{2,1,0:T(8,128)(2,1)S(1)}, bf16[1,128,2048]{2,1,0:T(8,128)(2,1)}, u32[]{:S(2)}) copy-start(bf16[1,128,2048]{2,1,0:T(8,128)(2,1)} %param.5) | copy-start | bytes 1572868
  45.7 22.5 %all-to-all-start.1 = ((bf16[32,2,4096]{2,1,0:T(2,128)(2,1)}), bf16[32,2,4096]{2,1,0:T(2,128)(2,1)S(1)}, u32[]{:S(2)}, u32[]{:S(2)}) async-start(bf16[32,2,4096]{2,1,0:T(2,128)(2,1)} %reshape.208), calls=%async_computation.1 | async-start | bytes 1048576 | tf_op jit(solution)/shard_map/all_to_all | solution.py:21
  54.2 1.0 copy-start.9
  57.0 1.6 copy-start.11
  74.0 1.9 copy-start
  75.9 1.4 copy-start.10
  75.9 1.4 copy-start.15
  77.3 1.7 copy-start.5
  83.2 32.9 %all-to-all-start.2 = ((f32[1,32,8192]{2,0,1:T(1,128)}), f32[1,32,8192]{2,0,1:T(1,128)}, u32[]{:S(2)}, u32[]{:S(2)}) async-start(f32[1,32,8192]{2,0,1:T(1,128)} %bitcast.93), calls=%async_computation.2 | async-start | bytes 2097152 | tf_op jit(solution)/shard_map/all_to_all | solution.py:13
  91.3 1.0 copy-start.4
  92.4 0.8 copy-start.2
  92.4 1.2 copy-start.1
  124.3 115.0 %all-to-all-start.3 = ((bf16[32,2,4096]{2,1,0:T(2,128)(2,1)}), bf16[32,2,4096]{2,1,0:T(2,128)(2,1)}, u32[]{:S(2)}, u32[]{:S(2)}) async-start(bf16[32,2,4096]{2,1,0:T(2,128)(2,1)} %reshape.210), calls=%async_computation.3 | async-start | bytes 1048576 | tf_op jit(solution)/shard_map/all_to_all | solution.py:21
  135.0 1.4 copy-start.8
  136.3 100.8 %copy-start.12 = (bf16[16,128,128]{2,1,0:T(8,128)(2,1)S(1)}, bf16[16,128,128]{2,1,0:T(8,128)(2,1)}, u32[]{:S(2)}) copy-start(bf16[16,128,128]{2,1,0:T(8,128)(2,1)} %copy-done.11) | copy-start | bytes 1572868
  237.2 1.2 copy-start.7
  248.2 1.2 copy-start.6
where the time goes:
time: 254 us; the launch traced here: 252 us
  blocking collectives  138 us (54%)
  waiting for transfers between devices  31.1 us (12%)
  local copies, waits for them, and re-layouts  26.8 us (11%)
  starting transfers between devices  24.8 us (10%)
  matrix products  15.8 us (6%)
  other arithmetic  15.3 us (6%)
    psum x1, blocking collectives, per_device(): total_gain = lax.psum(partial_gain, ('dp', 'seq'))  99.2 us
    all_to_all x1, blocking collectives, prefix_swapped(): lax.all_to_all(flat_state, 'seq', split_axis=1, concat_axis=0, tiled=True)  38.4 us
    all_to_all x1, waiting for transfers between devices, prefix_swapped(): lax.all_to_all(flat_state, 'seq', split_axis=1, concat_axis=0, tiled=True)  21.5 us
    all_to_all x2, starting transfers between devices, prefix_swapped(): lax.all_to_all(summed_half, 'seq', split_axis=0, concat_axis=1, tiled=True)  16.7 us
    unnamed x42, local copies, waits for them, and re-layouts  16.5 us
    all_to_all x4, other arithmetic, prefix_swapped(): lax.all_to_all(summed_half, 'seq', split_axis=0, concat_axis=1, tiled=True)  11.6 us
    all_to_all x2, waiting for transfers between devices, prefix_swapped(): lax.all_to_all(summed_half, 'seq', split_axis=0, concat_axis=1, tiled=True)  9.67 us
    all_to_all x1, starting transfers between devices, prefix_swapped(): lax.all_to_all(flat_state, 'seq', split_axis=1, concat_axis=0, tiled=True)  8.06 us
  transfers between devices with their start and end apart: 3, of which 2 were waited for; matrix products, arithmetic and copies ran while one was open for 5% of the time, Pallas kernels for 0%

commit v1 on v0

--- a/solution.py
+++ b/solution.py
@@ -49,7 +49,8 @@
     output = (gain * normalized).astype(jnp.bfloat16)[None]
     upstream = cotangent[0].astype(jnp.float32)
     partial_gain = jnp.sum(upstream * normalized, axis=0)
-    total_gain = lax.psum(partial_gain, ("dp", "seq"))
+    parts = lax.all_gather(partial_gain, ("dp", "seq"))
+    total_gain = jnp.sum(parts, axis=0)
     gain_grad = total_gain / lax.axis_size("dp")
     scaled = upstream * gain
     inner_mean = jnp.mean(scaled * normalized, axis=-1, keepdims=True)

time: 254 us -> 225 us (0.89)
  blocking collectives: 138 us -> 38.4 us
  waiting for transfers between devices: 31.1 us -> 79 us
  between operations: 0.88 us -> 14.2 us
  local copies, waits for them, and re-layouts: 26.8 us -> 30.9 us
  other arithmetic: 15.3 us -> 19 us
    psum x1 -> x0, blocking collectives: 99.2 us -> none  [per_device(): total_gain = lax.psum(partial_gain, ('dp', 'seq'))]
    all_gather x0 -> x1, waiting for transfers between devices: none -> 39.1 us  [per_device(): parts = lax.all_gather(partial_gain, ('dp', 'seq'))]
    all_to_all x2, waiting for transfers between devices: 9.67 us -> 20.6 us  [prefix_swapped(): lax.all_to_all(summed_half, 'seq', split_axis=0, concat_axis=1, tiled=True)]
    all_gather x0 -> x1, local copies, waits for them, and re-layouts: none -> 4.91 us  [per_device(): parts = lax.all_gather(partial_gain, ('dp', 'seq'))]
    unnamed x42 -> x20, local copies, waits for them, and re-layouts: 16.5 us -> 15.6 us
  transfers between devices with their start and end apart: 3 -> 4, of which waited for: 2 -> 4; matrix products, arithmetic and copies ran while one was open for 5% -> 18% of each run, Pallas kernels for 0% -> 0%
where the time goes in v1:
time: 225 us; the launch traced here: 224 us
  waiting for transfers between devices  79 us (35%)
  blocking collectives  38.4 us (17%)
  local copies, waits for them, and re-layouts  30.9 us (14%)
  starting transfers between devices  24.7 us (11%)
  other arithmetic  19 us (8%)
  matrix products  17.5 us (8%)
  between operations  14.2 us (6%)
    all_gather x1, waiting for transfers between devices, per_device(): parts = lax.all_gather(partial_gain, ('dp', 'seq'))  39.1 us
    all_to_all x1, blocking collectives, prefix_swapped(): lax.all_to_all(flat_state, 'seq', split_axis=1, concat_axis=0, tiled=True)  38.4 us
    all_to_all x2, waiting for transfers between devices, prefix_swapped(): lax.all_to_all(summed_half, 'seq', split_axis=0, concat_axis=1, tiled=True)  20.6 us
    all_to_all x1, waiting for transfers between devices, prefix_swapped(): lax.all_to_all(flat_state, 'seq', split_axis=1, concat_axis=0, tiled=True)  19.2 us
    all_to_all x2, starting transfers between devices, prefix_swapped(): lax.all_to_all(summed_half, 'seq', split_axis=0, concat_axis=1, tiled=True)  16.7 us
    unnamed x20, local copies, waits for them, and re-layouts  15.6 us
    all_to_all x4, other arithmetic, prefix_swapped(): lax.all_to_all(summed_half, 'seq', split_axis=0, concat_axis=1, tiled=True)  11 us
    all_to_all x1, starting transfers between devices, prefix_swapped(): lax.all_to_all(flat_state, 'seq', split_axis=1, concat_axis=0, tiled=True)  8.01 us
  transfers between devices with their start and end apart: 4, of which 4 were waited for; matrix products, arithmetic and copies ran while one was open for 18% of the time, Pallas kernels for 0%

profile of v1, /device:TPU:1, one launch (start us, length us, event | category | flops | bytes accessed | tf_op | source)
XLA Modules:
  0.0 223.6 jit_solution(3601339159602107984)
XLA Ops:
  10.3 38.4 %all_to_all.58 = f32[1,32,8192]{2,0,1:T(1,128)S(1)} all-to-all(f32[1,32,8192]{2,0,1:T(1,128)S(1)} %bitcast.94), channel_id=1, replica_groups=mesh['dp'=16,'seq'=32] {'seq'}, dimensions={1} | all-to-all | bytes 2097152 | tf_op jit(solution)/shard_map/all_to_all | solution.py:13
  48.6 1.3 fusion
  52.7 8.4 %all-to-all-start.1 = ((bf16[32,2,4096]{2,1,0:T(2,128)(2,1)}), bf16[32,2,4096]{2,1,0:T(2,128)(2,1)S(1)}, u32[]{:S(2)}, u32[]{:S(2)}) async-start(bf16[32,2,4096]{2,1,0:T(2,128)(2,1)} %reshape.209), calls=%async_computation.1 | async-start | bytes 1048576 | tf_op jit(solution)/shard_map/all_to_all | solution.py:21
  63.6 1.5 convolution_bitcast_fusion.3
  65.1 10.0 %all-to-all-done.1 = bf16[32,2,4096]{2,1,0:T(2,128)(2,1)S(1)} async-done(((bf16[32,2,4096]{2,1,0:T(2,128)(2,1)}), bf16[32,2,4096]{2,1,0:T(2,128)(2,1)S(1)}, u32[]{:S(2)}, u32[]{:S(2)}) %all-to-all-start.1) | async-done | bytes 524320 | tf_op jit(solution)/shard_map/all_to_all | solution.py:21
  75.6 4.0 %reduce.1 = bf16[32,8192]{1,0:T(8,128)(2,1)} reduce(bf16[32,1,8192]{2,1,0:T(2,128)(2,1)S(1)} %reshape.210, bf16[]{:T(256)} %constant.19), dimensions={1}, to_apply=%all_to_all.48.reduce_sub_computation | reduce | bytes 1048578 | tf_op jit(solution)/shard_map/all_to_all | solution.py:21
  79.6 1.3 reshape.200
  80.9 1.9 multiply_reduce_fusion
  82.8 1.3 copy.130
  84.1 2.4 %fusion.20 = (f32[2048]{0:T(1024)}, f32[128]{0:T(128)S(1)}) fusion(bf16[1,128,2048]{2,1,0:T(8,128)(2,1)} %param.9, f32[128,2048]{1,0:T(8,128)} %copy.130, f32[128]{0:T(128)S(1)} %add_sqrt_fusion, f32[2048]{0:T(1024)S(1)} %copy-done.4), kind=kLoop, calls=%fused_computation.34 | loop fusion | flops 1832832 | bytes 1590272 | tf_op jit(solution)/shard_map/reduce_sum | solution.py:51
  86.5 2.2 copy.129
  88.8 1.6 divide_convert_fusion
  90.3 1.3 fusion.3
  91.6 2.6 %copy.138 = f32[16,128,128]{2,1,0:T(8,128)} copy(f32[16,128,128]{1,2,0:T(8,128)} %fusion.3) | data formatting | bytes 2097152 | tf_op jit(solution)/shard_map/mul | solution.py:62
  94.2 8.0 %all-to-all-start.2 = ((f32[1,32,8192]{2,0,1:T(1,128)}), f32[1,32,8192]{2,0,1:T(1,128)}, u32[]{:S(2)}, u32[]{:S(2)}) async-start(f32[1,32,8192]{2,0,1:T(1,128)} %bitcast.93), calls=%async_computation.2 | async-start | bytes 2097152 | tf_op jit(solution)/shard_map/all_to_all | solution.py:13
  102.2 1.3 copy.128
  104.0 1.5 convolution_bitcast_fusion.2
  105.6 1.3 fusion.9
  107.9 19.2 %all-to-all-done.2 = f32[1,32,8192]{2,0,1:T(1,128)} async-done(((f32[1,32,8192]{2,0,1:T(1,128)}), f32[1,32,8192]{2,0,1:T(1,128)}, u32[]{:S(2)}, u32[]{:S(2)}) %all-to-all-start.2) | async-done | bytes 1048608 | tf_op jit(solution)/shard_map/all_to_all | solution.py:13
  127.1 2.4 %fusion.1 = bf16[32,1,8192]{2,0,1:T(8,128)(2,1)S(1)} fusion(f32[1,32,8192]{2,0,1:T(1,128)} %all-to-all-done.2), kind=kOutput, calls=%fused_computation.3 | convolution fusion | flops 100926464 | bytes 1572864 | tf_op jit(solution)/shard_map/dot_general | solution.py:19
  129.6 1.7 reduce.4
  131.3 2.2 reshape.211
  133.5 8.3 %all-to-all-start.3 = ((bf16[32,2,4096]{2,1,0:T(2,128)(2,1)}), bf16[32,2,4096]{2,1,0:T(2,128)(2,1)}, u32[]{:S(2)}, u32[]{:S(2)}) async-start(bf16[32,2,4096]{2,1,0:T(2,128)(2,1)} %reshape.211), calls=%async_computation.3 | async-start | bytes 1048576 | tf_op jit(solution)/shard_map/all_to_all | solution.py:21
  141.9 1.4 fusion.4
  143.2 1.3 fusion.34
  145.6 10.7 %all-to-all-done.3 = bf16[32,2,4096]{2,1,0:T(2,128)(2,1)} async-done(((bf16[32,2,4096]{2,1,0:T(2,128)(2,1)}), bf16[32,2,4096]{2,1,0:T(2,128)(2,1)}, u32[]{:S(2)}, u32[]{:S(2)}) %all-to-all-start.3) | async-done | bytes 524320 | tf_op jit(solution)/shard_map/all_to_all | solution.py:21
  156.2 4.4 %reshape.212 = bf16[32,1,8192]{2,1,0:T(2,128)(2,1)} reshape(bf16[32,2,4096]{2,1,0:T(2,128)(2,1)} %all-to-all-done.3) | data formatting | bytes 1048576
  160.7 4.3 %reduce.2 = bf16[32,8192]{1,0:T(8,128)(2,1)S(1)} reduce(bf16[32,1,8192]{2,1,0:T(2,128)(2,1)} %reshape.212, bf16[]{:T(256)} %constant.19), dimensions={1}, to_apply=%all_to_all.53.reduce_sub_computation | reduce | bytes 1048578 | tf_op jit(solution)/shard_map/all_to_all | solution.py:21
  165.2 1.7 fusion.12
  169.8 39.1 %all-gather.3.cloned.1.call-done = f32[1048576]{0:T(1024)} async-done(((f32[2048]{0:T(1024)}), f32[1048576]{0:T(1024)}) %all-gather.3.cloned.1.call-update) | async-done | bytes 4194320 | tf_op jit(solution)/shard_map/all_gather | solution.py:52
  208.9 4.9 %reshape.206 = f32[512,2048]{1,0:T(8,128)} reshape(f32[1048576]{0:T(1024)} %all-gather.3.cloned.1.call-done) | data formatting | bytes 8388608 | tf_op jit(solution)/shard_map/all_gather | solution.py:52
  213.8 2.4 %reduce_sum.39 = f32[2048]{0:T(1024)S(1)} reduce(f32[512,2048]{1,0:T(8,128)} %reshape.206, f32[]{:T(128)} %constant.4.clone.1), dimensions={0}, to_apply=%region_3.0 | reduce | flops 1046528 | bytes 4202500 | tf_op jit(solution)/shard_map/reduce_sum | solution.py:53
  (35 shorter events, 15.1 us)
Async XLA Ops:
  9.9 42.8 %copy-start.1 = (bf16[128,16,128]{0,2,1:T(8,128)(2,1)}, bf16[128,16,128]{0,2,1:T(8,128)(2,1)S(1)}, u32[]{:S(2)}) copy-start(bf16[128,16,128]{0,2,1:T(8,128)(2,1)S(1)} %copy.122) | copy-start | bytes 1572868
  52.7 22.3 %all-to-all-start.1 = ((bf16[32,2,4096]{2,1,0:T(2,128)(2,1)}), bf16[32,2,4096]{2,1,0:T(2,128)(2,1)S(1)}, u32[]{:S(2)}, u32[]{:S(2)}) async-start(bf16[32,2,4096]{2,1,0:T(2,128)(2,1)} %reshape.209), calls=%async_computation.1 | async-start | bytes 1048576 | tf_op jit(solution)/shard_map/all_to_all | solution.py:21
  61.1 147.8 %all-gather.3.cloned.1.call-start = ((), (), s32[]{:S(2)}) async-start(), calls=%async_computation.4 | async-start | bytes 4202496 | tf_op jit(solution)/shard_map/all_gather | solution.py:52
  62.8 0.8 copy-start.3
  75.6 8.5 %copy-start.4 = (f32[2048]{0:T(1024)S(1)}, f32[2048]{0:T(1024)}, u32[]{:S(2)}) copy-start(f32[2048]{0:T(1024)} %param.8) | copy-start | bytes 24580
  80.9 7.9 %copy-start = (bf16[16,128,128]{2,1,0:T(8,128)(2,1)}, bf16[16,128,128]{2,1,0:T(8,128)(2,1)S(1)}, u32[]{:S(2)}) copy-start(bf16[16,128,128]{2,1,0:T(8,128)(2,1)S(1)} %reshape.200) | copy-start | bytes 1572868
  94.2 33.0 %all-to-all-start.2 = ((f32[1,32,8192]{2,0,1:T(1,128)}), f32[1,32,8192]{2,0,1:T(1,128)}, u32[]{:S(2)}, u32[]{:S(2)}) async-start(f32[1,32,8192]{2,0,1:T(1,128)} %bitcast.93), calls=%async_computation.2 | async-start | bytes 2097152 | tf_op jit(solution)/shard_map/all_to_all | solution.py:13
  133.5 22.7 %all-to-all-start.3 = ((bf16[32,2,4096]{2,1,0:T(2,128)(2,1)}), bf16[32,2,4096]{2,1,0:T(2,128)(2,1)}, u32[]{:S(2)}, u32[]{:S(2)}) async-start(bf16[32,2,4096]{2,1,0:T(2,128)(2,1)} %reshape.211), calls=%async_computation.3 | async-start | bytes 1048576 | tf_op jit(solution)/shard_map/all_to_all | solution.py:21
  141.9 2.7 %copy-start.2 = (f32[1,128,2048]{2,1,0:T(8,128)S(1)}, f32[1,128,2048]{2,1,0:T(8,128)}, u32[]{:S(2)}) copy-start(f32[1,128,2048]{2,1,0:T(8,128)} %copy.128) | copy-start | bytes 3145732
Sparse Core Ops, SparseCore 0:
  86.6 122.1 all-gather.2
